TPU v7x, 256 devices: a whole 4x4x8 slice. The times are simulated.
256 devices in a mesh: dp: 16 (over z, core), mp: 16 (over y, x).
Axes of the slice: x: 4, y: 4, z: 8, core: 2. Of those that a mesh axis runs over, the one named last changes fastest.
Arguments:
- intermediate_signal: bfloat16 [16, 1024, 14336], P('mp', None, 'dp'), may hold values from -6 to 6
- frozen_down_weight: bfloat16 [14336, 4096], P('dp', 'mp'), may hold values from -0.046875 to 0.046875
- lowdim_entry_matrices: bfloat16 [16, 16, 14336, 64], P('mp', None, 'dp'), may hold values from -0.046875 to 0.046875
- lowdim_exit_matrices: bfloat16 [16, 16, 64, 4096], P('mp', 'dp'), may hold values from -0.75 to 0.75
- result_sensitivity: bfloat16 [16, 1024, 4096], P('mp', 'dp'), may hold values from -6 to 6
- token_client_choice: int32 [16, 1024], P('mp'), may hold values from 0 to 15, as said below
- matrix_bank_position: int32 [16, 16], P('mp'), may hold values from 0 to 15, as said below
- shard_active_entries: int32 [16, 16], P('mp'), may hold values from 32 to 64, as said below
Outputs:
- customized_projection_result: bfloat16 [16, 1024, 4096], P('mp', 'dp')
- entry_matrix_derivative: float32 [16, 16, 14336, 64], P('mp', None, 'dp')
- exit_matrix_derivative: float32 [16, 16, 64, 4096], P('mp', 'dp')
Inputs may be any that keep to these rules, and one draw needn't show every extreme that they name: `token_client_choice`: rows s * 64 to (s + 1) * 64 - 1 of a group belong to device s of dp. The owner of adapter u is matrix_bank_position[u]. Of one device's live rows at most 8 have adapters of one owner, and in every group one owner gets exactly 8 live rows from every device. `matrix_bank_position`: in each group a permutation of the slots. The live rows of a device are its first shard_active_entries rows; in each group some device has 64.
All inputs are finite; a program needn't handle non-finite values.
Results may differ from a plain program's by a relative error of at most 0.0065.
Values may be sent and summed in bfloat16 or wider, within the bound.
A program may use at most 128 MiB of HBM per device.

v0:
```python
import jax
import jax.numpy as jnp
from jax import lax
from jax.sharding import PartitionSpec as P


def route_tables(user_ids, slot_table, counts, tok_dev, capacity, adapters_per_device):
    dp_size = counts.shape[0]
    row_total = user_ids.shape[0]
    adapter_list = slot_table.shape[0]
    adapter_range = jnp.arange(adapter_list, dtype=jnp.int32)
    named = user_ids[:, None] == adapter_range[None, :]
    storage = jnp.sum(jnp.where(named, slot_table[None, :], 0), axis=1)
    row_ids = jnp.arange(row_total, dtype=jnp.int32)
    source_of = row_ids // tok_dev
    by_source = source_of[:, None] == jnp.arange(dp_size, dtype=jnp.int32)[None, :]
    row_limit = jnp.sum(jnp.where(by_source, counts[None, :], 0), axis=1)
    is_live = row_ids % tok_dev < row_limit
    owners = storage // adapters_per_device
    local_slot = storage % adapters_per_device
    owner_marks = (
        (owners[:, None] == jnp.arange(dp_size, dtype=jnp.int32)[None, :]) & is_live[:, None]
    ).astype(jnp.int32)
    per_source = owner_marks.reshape(dp_size, tok_dev, dp_size)
    earlier = jnp.cumsum(per_source, axis=1) - per_source
    row_rank = jnp.sum(earlier * per_source, axis=2)
    slot_hits = per_source[:, :, :, None] * (
        row_rank[:, :, None, None] == jnp.arange(capacity, dtype=jnp.int32)[None, None, None, :]
    ).astype(jnp.int32)
    filled = jnp.sum(slot_hits, axis=1)
    slot_row = (
        jnp.sum(slot_hits * jnp.arange(tok_dev, dtype=jnp.int32)[None, :, None, None], axis=1)
        + (1 - filled) * tok_dev
    )
    slot_adapter = jnp.sum(
        slot_hits * local_slot.reshape(dp_size, tok_dev)[:, :, None, None], axis=1
    )
    choose = ((storage[:, None] == adapter_range[None, :]) & is_live[:, None]).astype(jnp.float32)
    return (choose, slot_row, filled, slot_adapter)


def split_parts(values):
    upper = values.astype(jnp.bfloat16)
    lower = (values - upper.astype(jnp.float32)).astype(jnp.bfloat16)
    return (upper, lower)


def on_device(
    intermediate_signal,
    frozen_down_weight,
    lowdim_entry_matrices,
    lowdim_exit_matrices,
    result_sensitivity,
    token_client_choice,
    matrix_bank_position,
    shard_active_entries,
):
    my_index = lax.axis_index("dp")
    dp_size = lax.axis_size("dp")
    device_rows = intermediate_signal[0]
    row_total = device_rows.shape[0]
    tok_dev = row_total // dp_size
    capacity = tok_dev // 8
    adapters_per_device = lowdim_exit_matrices.shape[1]
    adapter_rank_width = lowdim_exit_matrices.shape[2]
    feature_count = lowdim_exit_matrices.shape[3]
    choose, slot_row, filled, slot_adapter = route_tables(
        token_client_choice[0],
        matrix_bank_position[0],
        shard_active_entries[0],
        tok_dev,
        capacity,
        adapters_per_device,
    )
    base_part = jnp.dot(
        device_rows,
        lax.all_gather(frozen_down_weight, "mp", axis=1, tiled=True),
        preferred_element_type=jnp.float32,
    )
    rank_everything = jnp.einsum(
        "xz,szu->xsu", device_rows, lowdim_entry_matrices[0], preferred_element_type=jnp.float32
    )
    rank_part = jnp.sum(rank_everything * choose[:, :, None], axis=1)
    base_own, rank_own = (
        lax.psum_scatter(base_part, "dp", scatter_dimension=0, tiled=True),
        lax.psum_scatter(rank_part, "dp", scatter_dimension=0, tiled=True),
    )
    my_slots = lax.dynamic_index_in_dim(slot_row, my_index, 0, keepdims=False)
    padded_rank = jnp.concatenate(
        [rank_own, jnp.zeros((1, adapter_rank_width), jnp.float32)], axis=0
    )
    padded_grad = jnp.concatenate(
        [result_sensitivity[0], jnp.zeros((1, feature_count), jnp.bfloat16)], axis=0
    )
    send_rank = padded_rank[my_slots]
    send_grad = padded_grad[my_slots].astype(jnp.float32)
    recv_rank, recv_grad = (
        lax.all_to_all(send_rank, "dp", split_axis=0, concat_axis=0, tiled=True),
        lax.all_to_all(send_grad, "dp", split_axis=0, concat_axis=0, tiled=True),
    )
    flat_rank = recv_rank.reshape(dp_size * capacity, adapter_rank_width)
    flat_grad = recv_grad.reshape(dp_size * capacity, feature_count).astype(jnp.bfloat16)
    mine_adapter = lax.dynamic_index_in_dim(slot_adapter, my_index, 1, keepdims=False).reshape(-1)
    mine_filled = lax.dynamic_index_in_dim(filled, my_index, 1, keepdims=False)
    marks = ((mine_adapter == 0) & (mine_filled.reshape(-1) > 0))[:, None]
    rank_upper, rank_lower = split_parts(flat_rank * marks.astype(jnp.float32))
    masked_grad = flat_grad * marks.astype(jnp.bfloat16)
    output_map_weight = lowdim_exit_matrices[0, 0]
    adapter_contribution = jnp.dot(
        rank_upper, output_map_weight, preferred_element_type=jnp.float32
    ) + jnp.dot(rank_lower, output_map_weight, preferred_element_type=jnp.float32)
    outer_dims = (((0,), (0,)), ((), ()))
    derivative_fragments = [
        lax.dot_general(rank_upper, flat_grad, outer_dims, preferred_element_type=jnp.float32)
        + lax.dot_general(rank_lower, flat_grad, outer_dims, preferred_element_type=jnp.float32)
    ]
    rank_back = lax.dot_general(
        masked_grad, output_map_weight, (((1,), (1,)), ((), ())), preferred_element_type=jnp.float32
    )
    exit_matrix_derivative = jnp.stack(derivative_fragments)[None]
    rank_grad = rank_back.reshape(dp_size, capacity, adapter_rank_width)
    returned = lax.all_to_all(
        adapter_contribution.reshape(dp_size, capacity, feature_count),
        "dp",
        split_axis=0,
        concat_axis=0,
        tiled=True,
    )
    placed = (
        jnp.zeros((tok_dev + 1, feature_count), jnp.float32)
        .at[my_slots.reshape(-1)]
        .add(returned.reshape(-1, feature_count))
    )
    total = base_own + placed[:tok_dev]
    customized_projection_result = total.astype(jnp.bfloat16)
    gathered = lax.all_gather(rank_grad[None], "dp", axis=0, tiled=True)
    owner_view = jnp.transpose(slot_row, (1, 0, 2))
    owner_filled = jnp.transpose(filled, (1, 0, 2))
    spots = jnp.where(
        owner_filled > 0,
        jnp.arange(dp_size, dtype=jnp.int32)[None, :, None] * tok_dev + owner_view,
        row_total,
    ).reshape(-1)
    rank_grad_rows = (
        jnp.zeros((row_total, adapter_rank_width), jnp.float32)
        .at[spots]
        .add(gathered.reshape(-1, adapter_rank_width), mode="drop")
    )
    grad_upper, grad_lower = split_parts(rank_grad_rows)
    choose_marks = choose.astype(jnp.bfloat16)[:, :, None]
    entry_matrix_derivative = jnp.einsum(
        "vg,vqh->qgh",
        device_rows,
        choose_marks * grad_upper[:, None, :],
        preferred_element_type=jnp.float32,
    )
    entry_matrix_derivative = entry_matrix_derivative + jnp.einsum(
        "vg,vqh->qgh",
        device_rows,
        choose_marks * grad_lower[:, None, :],
        preferred_element_type=jnp.float32,
    )
    return (
        customized_projection_result[None],
        entry_matrix_derivative[None],
        exit_matrix_derivative,
    )


def solution(mesh):
    in_specs = (
        P("mp", None, "dp"),
        P("dp", "mp"),
        P("mp", None, "dp", None),
        P("mp", "dp", None, None),
        P("mp", "dp", None),
        P("mp", None),
        P("mp", None),
        P("mp", None),
    )
    out_specs = (P("mp", "dp", None), P("mp", None, "dp", None), P("mp", "dp", None, None))
    return jax.shard_map(
        on_device, mesh=mesh, in_specs=in_specs, out_specs=out_specs, check_vma=False
    )
```

profile of v0, /device:TPU:1, one launch (start us, length us, event | category | flops | bytes accessed | tf_op | source)
XLA Modules:
  0.0 291.7 jit_solution(618486240489323896)
XLA Ops:
  8.1 0.7 all-gather.3.cloned.1.call-update
  8.8 0.8 select_reduce_fusion.2
  9.6 0.7 select_reduce_fusion.1
  10.4 0.6 fusion.48
  11.0 3.9 %fusion.11 = f32[1024,1024]{0,1:S(1)} fusion(bf16[896,1024]{0,1:T(8,128)(2,1)} %bitcast.91, bf16[1,1024,896]{2,1,0:T(8,128)(2,1)S(1)} %copy-done), kind=kOutput, calls=%fused_computation.20 | convolution fusion | flops 1879048192 | bytes 7864320
  15.4 1.0 copy.67
  16.6 74.1 %all-gather.3.cloned.1.call-done = bf16[896,4096]{1,0:T(8,128)(2,1)} async-done(((bf16[896,256]{1,0:T(8,128)(2,1)}), bf16[896,4096]{1,0:T(8,128)(2,1)}) %all-gather.3.cloned.1.call-update) | async-done | bytes 7340048 | tf_op jit(solution)/shard_map/all_gather | solution.py:77
  90.8 14.3 %fusion.13 = f32[1024,4096]{1,0:T(8,128)} fusion(bf16[896,4096]{1,0:T(8,128)(2,1)} %all-gather.3.cloned.1.call-done, bf16[1,1024,896]{2,1,0:T(8,128)(2,1)S(1)} %copy-done), kind=kOutput, calls=%fused_computation.22 | convolution fusion | flops 7516192768 | bytes 25952256 | tf_op jit(solution)/shard_map/dot_general | solution.py:75
  105.4 1.7 select_reduce_fusion
  107.8 8.7 %multiply_reduce_fusion.1 = (s32[16,16,8]{2,1,0:T(8,128)S(1)}, s32[16,16,8]{2,1,0:T(8,128)S(1)}) fusion(s32[16,64,8]{1,2,0:T(8,128)S(1)} %fusion.43, s32[16,64,16]{1,2,0:T(8,128)S(1)} %copy.65), kind=kLoop, calls=%fused_computation.24 | loop fusion | flops 520192 | bytes 114688 | tf_op jit(solution)/shard_map/reduce_sum | solution.py:30
  116.5 0.7 select_bitcast_fusion
  117.5 0.8 concatenate.6
  118.3 0.6 gather_fusion
  118.9 0.7 reshape.381
  119.7 9.1 %all-to-all-start = ((f32[16,1,512]{2,1,0:T(1,128)}), f32[16,1,512]{2,1,0:T(1,128)S(1)}, u32[]{:S(2)}, u32[]{:S(2)}) async-start(f32[16,1,512]{2,1,0:T(1,128)} %reshape.381), calls=%async_computation.2 | async-start | bytes 65536 | tf_op jit(solution)/shard_map/all_to_all | solution.py:98
  128.8 2.2 gather_fusion.1
  130.9 5.4 %all-to-all-done = f32[16,1,512]{2,1,0:T(1,128)S(1)} async-done(((f32[16,1,512]{2,1,0:T(1,128)}), f32[16,1,512]{2,1,0:T(1,128)S(1)}, u32[]{:S(2)}, u32[]{:S(2)}) %all-to-all-start) | async-done | bytes 32800 | tf_op jit(solution)/shard_map/all_to_all | solution.py:98
  136.9 3.9 %all-to-all-start.2 = ((bf16[16,8,4096]{2,1,0:T(8,128)(2,1)}), bf16[16,8,4096]{2,1,0:T(8,128)(2,1)S(1)}, u32[]{:S(2)}, u32[]{:S(2)}) async-start(bf16[16,8,4096]{2,1,0:T(8,128)(2,1)} %bitcast.84), calls=%async_computation.4 | async-start | bytes 2097152 | tf_op jit(solution)/shard_map/all_to_all | solution.py:99
  141.6 1.5 reduce
  143.6 1.8 fusion
  145.4 28.3 %all-to-all-done.2 = bf16[16,8,4096]{2,1,0:T(8,128)(2,1)S(1)} async-done(((bf16[16,8,4096]{2,1,0:T(8,128)(2,1)}), bf16[16,8,4096]{2,1,0:T(8,128)(2,1)S(1)}, u32[]{:S(2)}, u32[]{:S(2)}) %all-to-all-start.2) | async-done | bytes 1048608 | tf_op jit(solution)/shard_map/all_to_all | solution.py:99
  173.6 4.5 %all-to-all-start.1 = ((f32[16,8,4096]{2,1,0:T(8,128)}), f32[16,8,4096]{2,1,0:T(8,128)}, u32[]{:S(2)}, u32[]{:S(2)}) async-start(f32[16,8,4096]{2,1,0:T(8,128)} %fusion), calls=%async_computation.3 | async-start | bytes 4194304 | tf_op jit(solution)/shard_map/all_to_all | solution.py:122
  178.2 1.6 copy.72
  179.8 1.0 reshape.330
  181.4 75.7 %all-gather = f32[256,8,64]{2,1,0:T(8,128)} all-gather(f32[16,8,64]{2,1,0:T(8,128)S(1)} %fusion.25), channel_id=2, replica_groups=mesh['dp'=16,'mp'=16] {'dp'}, dimensions={0}, use_global_device_ids=true | all-gather | bytes 557056 | tf_op jit(solution)/shard_map/all_gather | solution.py:136
  257.1 11.0 %scatter_custom_fusion.1 = f32[1024,64]{1,0:T(8,128)S(1)} fusion(s32[2048]{0:T(1024)S(1)} %bitcast.87, f32[256,8,64]{2,1,0:T(8,128)} %all-gather, f32[]{:T(128)} %constant.81.clone.1), kind=kCustom, calls=%fused_computation.30 | custom fusion | flops 131072 | bytes 786436 | tf_op jit(solution)/shard_map/scatter-add | solution.py:147
  268.1 0.9 copy.74
  269.4 1.4 fusion.2
  270.9 2.3 fusion.5
  273.2 4.2 %add_bitcast_fusion = f32[1,16,896,64]{2,3,1,0:T(8,128)} fusion(f32[16,64,896]{2,1,0:T(8,128)S(1)} %fusion.5, bf16[1,1024,896]{2,1,0:T(8,128)(2,1)S(1)} %copy-done, bf16[1024,64]{0,1:T(8,128)(2,1)S(1)} %get-tuple-element.6, bf16[1024,16]{0,1:T(8,128)(2,1)S(1)} %copy-done.5), kind=kOutput, calls=%fused_computation.11 | convolution fusion | flops 1881014272 | bytes 9338880 | tf_op jit(solution)/shard_map/vg,vqh->qgh/dot_general | solution.py:151
  277.4 4.7 %scatter_custom_fusion = f32[65,4096]{1,0:T(8,128)S(1)} fusion(s32[128]{0:T(128)S(1)} %fusion.61, f32[16,8,4096]{2,1,0:T(8,128)} %all-to-all-done.1, f32[]{:T(128)} %constant.81.clone.1), kind=kCustom, calls=%fused_computation.12 | custom fusion | flops 524288 | bytes 3162116 | tf_op jit(solution)/shard_map/scatter-add | solution.py:132
  282.2 2.1 fusion.30
  (55 shorter events, 5.3 us)
Async XLA Ops:
  8.0 3.0 %copy-start = (bf16[1,1024,896]{2,1,0:T(8,128)(2,1)S(1)}, bf16[1,1024,896]{2,1,0:T(8,128)(2,1)}, u32[]{:S(2)}) copy-start(bf16[1,1024,896]{2,1,0:T(8,128)(2,1)} %param.8) | copy-start | bytes 5505028
  8.0 82.7 %all-gather.3.cloned.1.call-start = ((), (), s32[]{:S(2)}) async-start(), calls=%async_computation.5 | async-start | bytes 7798784 | tf_op jit(solution)/shard_map/all_gather | solution.py:77
  8.7 108.8 %reduce-scatter.5.cloned.1.call-start = ((), (), s32[]{:S(2)}) async-start(), calls=%async_computation.7 | async-start | bytes 557056 | tf_op jit(solution)/shard_map/reduce_scatter | solution.py:86
  16.4 265.8 %reduce-scatter.3.cloned.1.call-start = ((), (), s32[]{:S(2)}) async-start(), calls=%async_computation.6 | async-start | bytes 17825792 | tf_op jit(solution)/shard_map/reduce_scatter | solution.py:85
  105.0 23.7 %copy-start.3 = (bf16[1,64,4096]{2,1,0:T(8,128)(2,1)S(1)}, bf16[1,64,4096]{2,1,0:T(8,128)(2,1)}, u32[]{:S(2)}) copy-start(bf16[1,64,4096]{2,1,0:T(8,128)(2,1)} %param.12) | copy-start | bytes 1572868
  119.7 16.7 %all-to-all-start = ((f32[16,1,512]{2,1,0:T(1,128)}), f32[16,1,512]{2,1,0:T(1,128)S(1)}, u32[]{:S(2)}, u32[]{:S(2)}) async-start(f32[16,1,512]{2,1,0:T(1,128)} %reshape.381), calls=%async_computation.2 | async-start | bytes 65536 | tf_op jit(solution)/shard_map/all_to_all | solution.py:98
  130.9 12.2 %copy-start.1 = (bf16[1,1,64,4096]{3,2,1,0:T(8,128)(2,1)S(1)}, bf16[1,1,64,4096]{3,2,1,0:T(8,128)(2,1)}, u32[]{:S(2)}) copy-start(bf16[1,1,64,4096]{3,2,1,0:T(8,128)(2,1)} %param.11) | copy-start | bytes 1572868
  136.3 0.6 copy-start.4
  136.9 36.7 %all-to-all-start.2 = ((bf16[16,8,4096]{2,1,0:T(8,128)(2,1)}), bf16[16,8,4096]{2,1,0:T(8,128)(2,1)S(1)}, u32[]{:S(2)}, u32[]{:S(2)}) async-start(bf16[16,8,4096]{2,1,0:T(8,128)(2,1)} %bitcast.84), calls=%async_computation.4 | async-start | bytes 2097152 | tf_op jit(solution)/shard_map/all_to_all | solution.py:99
  173.6 103.8 %all-to-all-start.1 = ((f32[16,8,4096]{2,1,0:T(8,128)}), f32[16,8,4096]{2,1,0:T(8,128)}, u32[]{:S(2)}, u32[]{:S(2)}) async-start(f32[16,8,4096]{2,1,0:T(8,128)} %fusion), calls=%async_computation.3 | async-start | bytes 4194304 | tf_op jit(solution)/shard_map/all_to_all | solution.py:122
  269.4 1.4 copy-start.2
  269.4 1.4 copy-start.5
Sparse Core Ops, SparseCore 0:
  11.2 79.4 all-gather.2
Sparse Core Ops, SparseCore 1:
  16.5 59.3 reduce-scatter.4
  105.1 172.6 reduce-scatter.2
where the time goes:
time: 292 us
  waiting for transfers between devices  109 us (37%)
  blocking collectives  75.7 us (26%)
  other arithmetic  33.5 us (11%)
  matrix products  29.2 us (10%)
  starting transfers between devices  17.7 us (6%)
  between operations  15.7 us (5%)
  local copies, waits for them, and re-layouts  11.3 us (4%)
    all_gather x1, blocking collectives, on_device(): gathered = lax.all_gather(rank_grad[None], 'dp', axis=0, tiled=True)  75.7 us
    all_gather x1, waiting for transfers between devices, on_device(): lax.all_gather(frozen_down_weight, 'mp', axis=1, tiled=True)  74.1 us
    all_to_all x1, waiting for transfers between devices, on_device(): lax.all_to_all(send_grad, 'dp', split_axis=0, concat_axis=0, tiled=True)  28.3 us
    dot_general x1, matrix products, on_device(): jnp.dot(device_rows, lax.all_gather(frozen_down_weight, 'mp', axis=1, til...  14.3 us
    scatter-add x1, other arithmetic, on_device(): rank_grad_rows = jnp.zeros((row_total, adapter_rank_width), jnp.float32)....  11 us
    all_to_all x1, starting transfers between devices, on_device(): lax.all_to_all(send_rank, 'dp', split_axis=0, concat_axis=0, tiled=True)  9.05 us
    reduce_sum x1, other arithmetic, route_tables(): filled = jnp.sum(slot_hits, axis=1)  8.7 us
  transfers between devices with their start and end apart: 6, of which 3 were waited for; matrix products, arithmetic and copies ran while one was open for 24% of the time, Pallas kernels for 0%

commit v1 on v0

--- a/solution.py
+++ b/solution.py
@@ -74,7 +74,10 @@
     )
     base_part = jnp.dot(
         device_rows,
-        lax.all_gather(frozen_down_weight, "mp", axis=1, tiled=True),
+        jnp.concatenate(
+            lax.all_to_all(jnp.stack([frozen_down_weight] * lax.axis_size("mp")), "mp", 0, 0),
+            axis=1,
+        ),
         preferred_element_type=jnp.float32,
     )
     rank_everything = jnp.einsum(

time: 292 us -> 331 us (1.13)
  waiting for transfers between devices: 109 us -> 135 us
  starting transfers between devices: 17.7 us -> 26.6 us
  local copies, waits for them, and re-layouts: 11.3 us -> 16.7 us
    all_to_all x0 -> x1, waiting for transfers between devices: none -> 101 us  [on_device(): lax.all_to_all(jnp.stack([frozen_down_weight] * lax.axis_size('mp')), 'mp...]
    all_gather x1 -> x0, waiting for transfers between devices: 74.1 us -> none  [on_device(): lax.all_gather(frozen_down_weight, 'mp', axis=1, tiled=True)]
    all_to_all x0 -> x1, starting transfers between devices: none -> 7.75 us  [on_device(): lax.all_to_all(jnp.stack([frozen_down_weight] * lax.axis_size('mp')), 'mp...]
    another operation x0 -> x1, local copies, waits for them, and re-layouts: none -> 3.98 us  [on_device(): jnp.stack([frozen_down_weight] * lax.axis_size('mp'))]
  transfers between devices with their start and end apart: 6 -> 6, of which waited for: 3 -> 3; matrix products, arithmetic and copies ran while one was open for 24% -> 21% of each run, Pallas kernels for 0% -> 0%
where the time goes in v1:
time: 331 us; the launch traced here: 330 us
  waiting for transfers between devices  135 us (41%)
  blocking collectives  75.7 us (23%)
  other arithmetic  32.2 us (10%)
  matrix products  29.2 us (9%)
  starting transfers between devices  26.6 us (8%)
  local copies, waits for them, and re-layouts  16.7 us (5%)
  between operations  14.3 us (4%)
    all_to_all x1, waiting for transfers between devices, on_device(): lax.all_to_all(jnp.stack([frozen_down_weight] * lax.axis_size('mp')), 'mp...  101 us
    all_gather x1, blocking collectives, on_device(): gathered = lax.all_gather(rank_grad[None], 'dp', axis=0, tiled=True)  75.7 us
    all_to_all x1, waiting for transfers between devices, on_device(): lax.all_to_all(send_grad, 'dp', split_axis=0, concat_axis=0, tiled=True)  28.3 us
    dot_general x1, matrix products, on_device(): jnp.dot(device_rows, jnp.concatenate(lax.all_to_all(jnp.stack([frozen_dow...  14.3 us
    scatter-add x1, other arithmetic, on_device(): rank_grad_rows = jnp.zeros((row_total, adapter_rank_width), jnp.float32)....  11 us
    all_to_all x1, starting transfers between devices, on_device(): lax.all_to_all(send_rank, 'dp', split_axis=0, concat_axis=0, tiled=True)  10.2 us
    reduce_sum x1, other arithmetic, route_tables(): filled = jnp.sum(slot_hits, axis=1)  8.7 us
    all_to_all x1, starting transfers between devices, on_device(): lax.all_to_all(jnp.stack([frozen_down_weight] * lax.axis_size('mp')), 'mp...  7.75 us
  transfers between devices with their start and end apart: 6, of which 3 were waited for; matrix products, arithmetic and copies ran while one was open for 21% of the time, Pallas kernels for 0%

profile of v1, /device:TPU:1, one launch (start us, length us, event | category | flops | bytes accessed | tf_op | source)
XLA Modules:
  0.0 329.9 jit_solution(4218074610942494179)
XLA Ops:
  7.2 1.4 copy.66
  8.6 4.0 %stack.2 = bf16[16,896,256]{1,2,0:T(8,128)(2,1)} broadcast(bf16[896,256]{0,1:T(8,128)(2,1)S(1)} %copy.66), dimensions={1,2} | broadcast | bytes 7798784 | tf_op jit(solution)/shard_map/stack | solution.py:78
  12.6 7.7 %all-to-all-start = ((bf16[16,896,256]{1,2,0:T(8,128)(2,1)}), bf16[16,896,256]{1,2,0:T(8,128)(2,1)}, u32[]{:S(2)}, u32[]{:S(2)}) async-start(bf16[16,896,256]{1,2,0:T(8,128)(2,1)} %stack.2), calls=%async_computation | async-start | bytes 14680064 | tf_op jit(solution)/shard_map/all_to_all | solution.py:78
  20.6 0.6 fusion.48
  21.2 3.9 %fusion.11 = f32[1024,1024]{0,1:S(1)} fusion(bf16[896,1024]{0,1:T(8,128)(2,1)} %bitcast.94, bf16[1,1024,896]{2,1,0:T(8,128)(2,1)S(1)} %copy-done), kind=kOutput, calls=%fused_computation.20 | convolution fusion | flops 1879048192 | bytes 7864320
  25.6 1.0 copy.71
  26.9 101.5 %all-to-all-done = bf16[16,896,256]{1,2,0:T(8,128)(2,1)} async-done(((bf16[16,896,256]{1,2,0:T(8,128)(2,1)}), bf16[16,896,256]{1,2,0:T(8,128)(2,1)}, u32[]{:S(2)}, u32[]{:S(2)}) %all-to-all-start) | async-done | bytes 7340064 | tf_op jit(solution)/shard_map/all_to_all | solution.py:78
  128.3 14.3 %fusion.13 = f32[1024,4096]{1,0:T(8,128)} fusion(bf16[896,4096]{0,1:T(8,128)(2,1)} %bitcast.2, bf16[1,1024,896]{2,1,0:T(8,128)(2,1)S(1)} %copy-done), kind=kOutput, calls=%fused_computation.22 | convolution fusion | flops 7516192768 | bytes 25952256 | tf_op jit(solution)/shard_map/dot_general | solution.py:75
  143.0 1.7 select_reduce_fusion
  145.4 8.7 %multiply_reduce_fusion.1 = (s32[16,16,8]{2,1,0:T(8,128)S(1)}, s32[16,16,8]{2,1,0:T(8,128)S(1)}) fusion(s32[16,64,8]{1,2,0:T(8,128)S(1)} %fusion.43, s32[16,64,16]{1,2,0:T(8,128)S(1)} %copy.69), kind=kLoop, calls=%fused_computation.24 | loop fusion | flops 520192 | bytes 114688 | tf_op jit(solution)/shard_map/reduce_sum | solution.py:30
  154.1 0.7 select_bitcast_fusion
  155.1 0.8 concatenate.6
  155.9 0.6 gather_fusion
  156.5 0.7 reshape.391
  157.3 10.2 %all-to-all-start.1 = ((f32[16,1,512]{2,1,0:T(1,128)}), f32[16,1,512]{2,1,0:T(1,128)S(1)}, u32[]{:S(2)}, u32[]{:S(2)}) async-start(f32[16,1,512]{2,1,0:T(1,128)} %reshape.391), calls=%async_computation.3 | async-start | bytes 65536 | tf_op jit(solution)/shard_map/all_to_all | solution.py:101
  167.6 2.2 gather_fusion.1
  169.7 5.4 %all-to-all-done.1 = f32[16,1,512]{2,1,0:T(1,128)S(1)} async-done(((f32[16,1,512]{2,1,0:T(1,128)}), f32[16,1,512]{2,1,0:T(1,128)S(1)}, u32[]{:S(2)}, u32[]{:S(2)}) %all-to-all-start.1) | async-done | bytes 32800 | tf_op jit(solution)/shard_map/all_to_all | solution.py:101
  175.7 3.9 %all-to-all-start.3 = ((bf16[16,8,4096]{2,1,0:T(8,128)(2,1)}), bf16[16,8,4096]{2,1,0:T(8,128)(2,1)S(1)}, u32[]{:S(2)}, u32[]{:S(2)}) async-start(bf16[16,8,4096]{2,1,0:T(8,128)(2,1)} %bitcast.87), calls=%async_computation.5 | async-start | bytes 2097152 | tf_op jit(solution)/shard_map/all_to_all | solution.py:102
  180.3 1.5 reduce
  182.3 1.8 fusion
  184.1 28.3 %all-to-all-done.3 = bf16[16,8,4096]{2,1,0:T(8,128)(2,1)S(1)} async-done(((bf16[16,8,4096]{2,1,0:T(8,128)(2,1)}), bf16[16,8,4096]{2,1,0:T(8,128)(2,1)S(1)}, u32[]{:S(2)}, u32[]{:S(2)}) %all-to-all-start.3) | async-done | bytes 1048608 | tf_op jit(solution)/shard_map/all_to_all | solution.py:102
  212.4 4.5 %all-to-all-start.2 = ((f32[16,8,4096]{2,1,0:T(8,128)}), f32[16,8,4096]{2,1,0:T(8,128)}, u32[]{:S(2)}, u32[]{:S(2)}) async-start(f32[16,8,4096]{2,1,0:T(8,128)} %fusion), calls=%async_computation.4 | async-start | bytes 4194304 | tf_op jit(solution)/shard_map/all_to_all | solution.py:125
  217.0 1.6 copy.76
  218.6 1.0 reshape.340
  220.2 75.7 %all-gather = f32[256,8,64]{2,1,0:T(8,128)} all-gather(f32[16,8,64]{2,1,0:T(8,128)S(1)} %fusion.25), channel_id=2, replica_groups=mesh['dp'=16,'mp'=16] {'dp'}, dimensions={0}, use_global_device_ids=true | all-gather | bytes 557056 | tf_op jit(solution)/shard_map/all_gather | solution.py:139
  295.9 11.0 %scatter_custom_fusion.1 = f32[1024,64]{1,0:T(8,128)S(1)} fusion(s32[2048]{0:T(1024)S(1)} %bitcast.90, f32[256,8,64]{2,1,0:T(8,128)} %all-gather, f32[]{:T(128)} %constant.81.clone.1), kind=kCustom, calls=%fused_computation.30 | custom fusion | flops 131072 | bytes 786436 | tf_op jit(solution)/shard_map/scatter-add | solution.py:150
  306.9 0.9 copy.78
  308.2 1.4 fusion.2
  309.6 2.3 fusion.5
  312.0 4.2 %add_bitcast_fusion = f32[1,16,896,64]{2,3,1,0:T(8,128)} fusion(f32[16,64,896]{2,1,0:T(8,128)S(1)} %fusion.5, bf16[1,1024,896]{2,1,0:T(8,128)(2,1)S(1)} %copy-done, bf16[1024,64]{0,1:T(8,128)(2,1)S(1)} %get-tuple-element.6, bf16[1024,16]{0,1:T(8,128)(2,1)S(1)} %copy-done.5), kind=kOutput, calls=%fused_computation.11 | convolution fusion | flops 1881014272 | bytes 9338880 | tf_op jit(solution)/shard_map/vg,vqh->qgh/dot_general | solution.py:154
  316.2 4.8 %scatter_custom_fusion = f32[65,4096]{1,0:T(8,128)S(1)} fusion(s32[128]{0:T(128)S(1)} %fusion.61, f32[16,8,4096]{2,1,0:T(8,128)} %all-to-all-done.2, f32[]{:T(128)} %constant.81.clone.1), kind=kCustom, calls=%fused_computation.12 | custom fusion | flops 524288 | bytes 3162116 | tf_op jit(solution)/shard_map/scatter-add | solution.py:135
  321.0 2.1 fusion.30
  (62 shorter events, 5.4 us)
Async XLA Ops:
  7.2 14.1 %copy-start = (bf16[1,1024,896]{2,1,0:T(8,128)(2,1)S(1)}, bf16[1,1024,896]{2,1,0:T(8,128)(2,1)}, u32[]{:S(2)}) copy-start(bf16[1,1024,896]{2,1,0:T(8,128)(2,1)} %param.8) | copy-start | bytes 5505028
  12.6 7.8 %copy-start.6 = (s32[1,1024]{1,0:T(1,128)S(1)}, s32[1,1024]{1,0:T(1,128)}, u32[]{:S(2)}) copy-start(s32[1,1024]{1,0:T(1,128)} %param.13) | copy-start | bytes 12292
  12.6 7.8 %copy-start.7 = (s32[1,16]{1,0:T(1,128)S(1)}, s32[1,16]{1,0:T(1,128)}, u32[]{:S(2)}) copy-start(s32[1,16]{1,0:T(1,128)} %param.14) | copy-start | bytes 196
  12.6 7.9 %copy-start.8 = (s32[1,16]{1,0:T(1,128)S(1)}, s32[1,16]{1,0:T(1,128)}, u32[]{:S(2)}) copy-start(s32[1,16]{1,0:T(1,128)} %param.15) | copy-start | bytes 196
  12.6 115.7 %all-to-all-start = ((bf16[16,896,256]{1,2,0:T(8,128)(2,1)}), bf16[16,896,256]{1,2,0:T(8,128)(2,1)}, u32[]{:S(2)}, u32[]{:S(2)}) async-start(bf16[16,896,256]{1,2,0:T(8,128)(2,1)} %stack.2), calls=%async_computation | async-start | bytes 14680064 | tf_op jit(solution)/shard_map/all_to_all | solution.py:78
  20.3 134.8 %reduce-scatter.5.cloned.1.call-start = ((), (), s32[]{:S(2)}) async-start(), calls=%async_computation.7 | async-start | bytes 557056 | tf_op jit(solution)/shard_map/reduce_scatter | solution.py:89
  26.6 294.4 %reduce-scatter.3.cloned.1.call-start = ((), (), s32[]{:S(2)}) async-start(), calls=%async_computation.6 | async-start | bytes 17825792 | tf_op jit(solution)/shard_map/reduce_scatter | solution.py:88
  142.7 24.9 %copy-start.3 = (bf16[1,64,4096]{2,1,0:T(8,128)(2,1)S(1)}, bf16[1,64,4096]{2,1,0:T(8,128)(2,1)}, u32[]{:S(2)}) copy-start(bf16[1,64,4096]{2,1,0:T(8,128)(2,1)} %param.12) | copy-start | bytes 1572868
  157.3 17.8 %all-to-all-start.1 = ((f32[16,1,512]{2,1,0:T(1,128)}), f32[16,1,512]{2,1,0:T(1,128)S(1)}, u32[]{:S(2)}, u32[]{:S(2)}) async-start(f32[16,1,512]{2,1,0:T(1,128)} %reshape.391), calls=%async_computation.3 | async-start | bytes 65536 | tf_op jit(solution)/shard_map/all_to_all | solution.py:101
  169.7 12.1 %copy-start.1 = (bf16[1,1,64,4096]{3,2,1,0:T(8,128)(2,1)S(1)}, bf16[1,1,64,4096]{3,2,1,0:T(8,128)(2,1)}, u32[]{:S(2)}) copy-start(bf16[1,1,64,4096]{3,2,1,0:T(8,128)(2,1)} %param.11) | copy-start | bytes 1572868
  175.1 0.6 copy-start.4
  175.7 36.7 %all-to-all-start.3 = ((bf16[16,8,4096]{2,1,0:T(8,128)(2,1)}), bf16[16,8,4096]{2,1,0:T(8,128)(2,1)S(1)}, u32[]{:S(2)}, u32[]{:S(2)}) async-start(bf16[16,8,4096]{2,1,0:T(8,128)(2,1)} %bitcast.87), calls=%async_computation.5 | async-start | bytes 2097152 | tf_op jit(solution)/shard_map/all_to_all | solution.py:102
  212.4 103.8 %all-to-all-start.2 = ((f32[16,8,4096]{2,1,0:T(8,128)}), f32[16,8,4096]{2,1,0:T(8,128)}, u32[]{:S(2)}, u32[]{:S(2)}) async-start(f32[16,8,4096]{2,1,0:T(8,128)} %fusion), calls=%async_computation.4 | async-start | bytes 4194304 | tf_op jit(solution)/shard_map/all_to_all | solution.py:125
  308.2 1.4 copy-start.2
  308.2 1.4 copy-start.5
Sparse Core Ops, SparseCore 0:
  26.7 59.9 reduce-scatter.4
  142.8 174.3 reduce-scatter.2
